TPU v7x, 512 devices: a whole 4x4x16 slice. The times are simulated.
512 devices in a mesh: shot: 16 (over z_hi, y), slab: 32 (over z_lo, x, core).
Axes of the slice: x: 4, y: 4, z: 16 (z_hi: 4, z_lo: 4; z = z_hi * 4 + z_lo), core: 2. Of those that a mesh axis runs over, the one named last changes fastest.
Arguments:
- wave_now: float32 [16, 512, 64, 128], P('shot', 'slab'), may hold values from -6 to 6
- wave_prev: float32 [16, 512, 64, 128], P('shot', 'slab'), may hold values from -6 to 6
- courant: float32 [512, 64, 128], P('slab'), may hold values from 0.05 to 0.2
- forward: bfloat16 [16, 3, 512, 64, 128], P('shot', None, 'slab'), may hold values from -6 to 6
- receivers: int32 [16, 3, 256], P('shot'), may hold values from 0 to 511, as said below
- residual: float32 [16, 3, 256], P('shot'), may hold values from -6 to 6
- aperture: int32 [16, 2], P('shot'), may hold values from 0 to 512, as said below
- latent: bfloat16 [256, 32, 4096], P('slab', 'shot')
- weight: float32 [64, 8], replicated, may hold values from -0.75 to 0.75
Outputs:
- wave_after: float32 [16, 512, 64, 128], P('shot', 'slab')
- wave_before: float32 [16, 512, 64, 128], P('shot', 'slab')
- latent_grad: float32 [256, 32, 4096], P('slab', 'shot')
- weight_grad: float32 [64, 8], replicated
Inputs may be any that keep to these rules, and one draw needn't show every extreme that they name: receivers[s,0,r], receivers[s,1,r], receivers[s,2,r] are an x, y and depth cell inside the grid. Each shot's aperture is a range of at least 512 // 4 x cells with aperture[s,0] < aperture[s,1].
All inputs are finite; a program needn't handle non-finite values.
Results may differ from a plain program's by a relative error of at most 0.0003.
Values sent between devices are 32-bit elements; how exact they have to be, the bound alone decides.
No kernel may reach another device: no remote copies, remote signals or barrier semaphores. Data moves between devices by JAX's collectives and lax.ppermute only.
A program may use at most 64 MiB of HBM per device.

v0:
```python
import math
import jax
import jax.numpy as jnp
from jax import lax
from jax.sharding import PartitionSpec as P

STEPS = 3
stencil_weights = (-205.0 / 72.0, 8.0 / 5.0, -1.0 / 5.0, 8.0 / 315.0, -1.0 / 560.0)


def extended(block, sides, width):
    for axis, dim in sides:
        count = lax.axis_size(axis)
        forward = [(i, i + 1) for i in range(count - 1)]
        backward = [(target, source) for source, target in forward]
        low = lax.ppermute(
            lax.slice_in_dim(block, block.shape[dim] - width, None, axis=dim), axis, forward
        )
        high = lax.ppermute(lax.slice_in_dim(block, 0, width, axis=dim), axis, backward)
        block = jnp.concatenate([low, block, high], axis=dim)
    return block


def laplace(padded):
    size_x = padded.shape[0] - 8
    size_y = padded.shape[1] - 8
    size_z = padded.shape[2] - 8

    def moved(shift_x, shift_y, shift_z):
        return padded[
            4 + shift_x : 4 + shift_x + size_x,
            4 + shift_y : 4 + shift_y + size_y,
            4 + shift_z : 4 + shift_z + size_z,
        ]

    total = 3.0 * stencil_weights[0] * moved(0, 0, 0)
    for offset in range(1, 5):
        cycle_sum = moved(offset, 0, 0) + moved(-offset, 0, 0)
        cycle_sum = cycle_sum + moved(0, offset, 0) + moved(0, -offset, 0)
        cycle_sum = cycle_sum + moved(0, 0, offset) + moved(0, 0, -offset)
        total = total + stencil_weights[offset] * cycle_sum
    return total


def pad_sides(field):
    return jnp.pad(field, ((0, 0), (4, 4), (4, 4)))


def inject(field, receivers, values, first_x):
    extent = field.shape[0]
    local_x = receivers[0, 0] - first_x
    valid = (local_x >= 0) & (local_x < extent)
    local_x = jnp.where(valid, local_x, extent)
    return field.at[local_x, receivers[0, 1], receivers[0, 2]].add(values, mode="drop")


def body(wave_now, wave_prev, courant, forward, receivers, residual, aperture, latent, weight):
    slab_cells = courant.shape[0]
    first_x = lax.axis_index("slab") * slab_cells
    current = wave_now[0]
    previous = wave_prev[0]
    accum = jnp.zeros(current.shape, jnp.float32)
    for instant in range(STEPS):
        padded = extended(current, (("slab", 0),), 4)
        advanced = 2.0 * current - previous + courant * laplace(pad_sides(padded))
        advanced = inject(advanced, receivers, residual[0, instant], first_x)
        accum = accum + advanced * forward[0, instant].astype(jnp.float32)
        previous = current
        current = advanced
    x_cells = first_x + jnp.arange(slab_cells, dtype=jnp.int32)
    inside = (x_cells >= aperture[0, 0]) & (x_cells < aperture[0, 1])
    image = jnp.where(inside[:, None, None], courant * accum, 0.0)
    image_rows = image.transpose(1, 0, 2)
    tile_rows = image_rows.shape[0] // lax.axis_size("shot")
    tile = lax.psum_scatter(image_rows, "shot", scatter_dimension=0, tiled=True).transpose(1, 0, 2)
    half_x = slab_cells // 2
    half_y = tile_rows // 2
    half_z = tile.shape[2] // 2
    taps = (
        tile.reshape(half_x, 2, half_y, 2, half_z, 2)
        .transpose(0, 2, 4, 1, 3, 5)
        .reshape(half_x, half_y, half_z, 8)
    )
    channels = weight.shape[0]
    latent_grad = jnp.einsum(
        "ijkq,cq->ijck", taps, weight, precision=lax.Precision.HIGHEST
    ).reshape(half_x, half_y, channels * half_z)
    latent_wide = latent.astype(jnp.float32).reshape(half_x, half_y, channels, half_z)
    partial_grad = jnp.einsum("ijck,ijkq->cq", latent_wide, taps, precision=lax.Precision.HIGHEST)
    latent_cells = (
        latent.shape[0] * lax.axis_size("slab") * latent.shape[1] * lax.axis_size("shot") * half_z
    )
    weight_grad = lax.psum(partial_grad, ("shot", "slab")) * (1.0 / math.sqrt(latent_cells))
    return (current[None], previous[None], latent_grad, weight_grad)


def solution(mesh):
    return jax.shard_map(
        body,
        mesh=mesh,
        in_specs=(
            P("shot", "slab", None, None),
            P("shot", "slab", None, None),
            P("slab", None, None),
            P("shot", None, "slab", None, None),
            P("shot", None, None),
            P("shot", None, None),
            P("shot", None),
            P("slab", "shot", None),
            P(),
        ),
        out_specs=(
            P("shot", "slab", None, None),
            P("shot", "slab", None, None),
            P("slab", "shot", None),
            P(),
        ),
        check_vma=False,
    )
```

profile of v0, /device:TPU:1, one launch (start us, length us, event | category | flops | bytes accessed | tf_op | source)
XLA Modules:
  0.0 334.7 jit_solution(5647150959445888792)
XLA Ops:
  7.2 1.1 slice_bitcast_fusion.1
  8.3 8.8 %collective-permute-start = (f32[4,64,128]{2,1,0:T(8,128)S(1)}, f32[4,64,128]{2,1,0:T(8,128)S(1)}, u32[]{:S(2)}, u32[]{:S(2)}) collective-permute-start(f32[4,64,128]{2,1,0:T(8,128)S(1)} %get-tuple-element.24), channel_id=1, source_target_pairs={{1,0},{2,1},{3,2},{4,3},{5,4},{6,5},{7,6},{8,7},{9,8},{10,9},{11,1... | collective-permute-start | bytes 393224 | tf_op jit(solution)/shard_map/ppermute | solution.py:19
  17.1 1.9 collective-permute-start.1
  19.0 0.7 fusion.67
  19.8 0.7 or_select_fusion
  20.5 0.5 collective-permute-done.1
  21.0 0.7 copy-done.6
  21.6 1.6 select_maximum_fusion.4
  23.2 3.7 %fusion.13 = f32[16,64,128]{2,1,0:T(8,128)S(1)} fusion(f32[16,64,128]{2,1,0:T(8,128)S(1)} %copy-done.3, f32[16,64,128]{2,1,0:T(8,128)S(1)} %bitcast.63, f32[4,64,128]{2,1,0:T(8,128)} %copy-done.6, f32[4,64,128]{2,1,0:T(8,128)S(1)} %collective-permute-done, f32[24,72,136]{2,1,0:T(8,128)S(1)} %select_maximum_fusion.4, f32[1,16,64,128]{3,2,1,0:T(8,128)} %param.10), kind=kLoop, calls=%fused_computation.40 | loop fusion | flops 5373952 | bytes 10747904 | tf_op jit(solution)/shard_map/add | solution.py:65
  26.9 15.6 %scatter_fusion = f32[16,64,128]{2,1,0:T(8,128)S(1)} fusion(f32[16,64,128]{2,1,0:T(8,128)S(1)} %fusion.13, s32[256]{0:T(256)S(1)} %bitcast.56, f32[256]{0:T(256)S(1)} %bitcast.69), kind=kCustom, calls=%fused_computation | custom fusion | flops 256 | bytes 6144 | tf_op jit(solution)/shard_map/scatter-add | solution.py:54
  42.5 4.3 %collective-permute-start.3 = (f32[4,64,128]{2,1,0:T(8,128)S(1)}, f32[4,64,128]{2,1,0:T(8,128)S(1)}, u32[]{:S(2)}, u32[]{:S(2)}) collective-permute-start(f32[4,64,128]{2,1,0:T(8,128)S(1)} %get-tuple-element.22), channel_id=1, source_target_pairs={{0,1},{1,2},{2,3},{3,4},{4,5},{5,6},{6,7},{7,8},{8,9},{9,10},{10,1... | collective-permute-start | bytes 393224 | tf_op jit(solution)/shard_map/ppermute | solution.py:16
  46.8 1.9 collective-permute-start.2
  48.9 4.2 %collective-permute-done.2 = f32[4,64,128]{2,1,0:T(8,128)S(1)} collective-permute-done((f32[4,64,128]{2,1,0:T(8,128)S(1)}, f32[4,64,128]{2,1,0:T(8,128)S(1)}, u32[]{:S(2)}, u32[]{:S(2)}) %collective-permute-start.2) | collective-permute-done | bytes 131104 | tf_op jit(solution)/shard_map/ppermute | solution.py:19
  53.1 0.5 select_maximum_fusion.2
  53.7 2.1 fusion.46
  55.8 15.6 %scatter_fusion.1 = f32[16,64,128]{2,1,0:T(8,128)S(1)} fusion(f32[16,64,128]{2,1,0:T(8,128)S(1)} %fusion.46, s32[256]{0:T(256)S(1)} %bitcast.57, f32[256]{0:T(256)S(1)} %bitcast.68), kind=kCustom, calls=%fused_computation.1 | custom fusion | flops 256 | bytes 6144 | tf_op jit(solution)/shard_map/scatter-add | solution.py:54
  71.4 1.9 collective-permute-start.5
  73.3 0.6 fusion.68
  73.9 1.3 compare_and_fusion
  75.2 2.6 collective-permute-start.4
  78.0 3.5 %collective-permute-done.4 = f32[4,64,128]{2,1,0:T(8,128)S(1)} collective-permute-done((f32[4,64,128]{2,1,0:T(8,128)S(1)}, f32[4,64,128]{2,1,0:T(8,128)S(1)}, u32[]{:S(2)}, u32[]{:S(2)}) %collective-permute-start.4) | collective-permute-done | bytes 131104 | tf_op jit(solution)/shard_map/ppermute | solution.py:19
  81.5 0.5 select_maximum_fusion
  82.1 2.1 fusion.36
  84.2 15.6 %scatter_fusion.2 = f32[16,64,128]{2,1,0:T(8,128)S(1)} fusion(f32[16,64,128]{2,1,0:T(8,128)S(1)} %fusion.36, s32[256]{0:T(256)S(1)} %bitcast.58, f32[256]{0:T(256)S(1)} %bitcast.67), kind=kCustom, calls=%fused_computation.2 | custom fusion | flops 256 | bytes 6144 | tf_op jit(solution)/shard_map/scatter-add | solution.py:54
  100.1 1.1 copy.23
  101.4 118.1 %reduce-scatter.2.cloned.1.call-done = f32[4,16,128]{2,1,0:T(8,128)} async-done(((f32[64,16,128]{2,1,0:T(8,128)}), f32[4,16,128]{2,1,0:T(8,128)}) %reduce-scatter.2.cloned.1.call-update) | async-done | bytes 32784 | tf_op jit(solution)/shard_map/reduce_scatter | solution.py:75
  219.6 2.8 reshape.124
  222.4 0.7 copy.24
  223.1 1.0 convolution_bitcast_fusion
  224.3 1.0 reshape.151
  225.6 101.6 %psum.7 = f32[64,8]{0,1:T(8,128)S(1)} all-reduce(f32[64,8]{0,1:T(8,128)S(1)} %convolution_bitcast_fusion.1), channel_id=1, replica_groups=mesh['shot'=16,'slab'=32] {'shot','slab'}, use_global_device_ids=true, to_apply=%region_4.5 | all-reduce | flops 512 | bytes 4096 | tf_op jit(solution)/shard_map/psum | solution.py:93
  327.2 0.6 broadcast_multiply_fusion
  (34 shorter events, 1.4 us)
Async XLA Ops:
  7.2 215.9 %copy-start = (f32[64,8]{0,1:T(8,128)S(1)}, f32[64,8]{0,1:T(8,128)}, u32[]{:S(2)}) copy-start(f32[64,8]{0,1:T(8,128)} %param.17) | copy-start | bytes 6148
  7.2 16.0 %copy-start.4 = (f32[1,16,64,128]{3,2,1,0:T(8,128)S(1)}, f32[1,16,64,128]{3,2,1,0:T(8,128)}, u32[]{:S(2)}) copy-start(f32[1,16,64,128]{3,2,1,0:T(8,128)} %param.9) | copy-start | bytes 1572868
  7.2 16.0 %copy-start.3 = (f32[16,64,128]{2,1,0:T(8,128)S(1)}, f32[16,64,128]{2,1,0:T(8,128)}, u32[]{:S(2)}) copy-start(f32[16,64,128]{2,1,0:T(8,128)} %param.11) | copy-start | bytes 1572868
  7.2 212.3 %reduce-scatter.2.cloned.1.call-start = ((), (), s32[]{:S(2)}) async-start(), calls=%async_computation.1 | async-start | bytes 557056 | tf_op jit(solution)/shard_map/reduce_scatter | solution.py:75
  8.3 12.2 %collective-permute-start = (f32[4,64,128]{2,1,0:T(8,128)S(1)}, f32[4,64,128]{2,1,0:T(8,128)S(1)}, u32[]{:S(2)}, u32[]{:S(2)}) collective-permute-start(f32[4,64,128]{2,1,0:T(8,128)S(1)} %get-tuple-element.24), channel_id=1, source_target_pairs={{1,0},{2,1},{3,2},{4,3},{5,4},{6,5},{7,6},{8,7},{9,8},{10,9},{11,1... | collective-permute-start | bytes 393224 | tf_op jit(solution)/shard_map/ppermute | solution.py:19
  17.1 3.9 %collective-permute-start.1 = (f32[4,64,128]{2,1,0:T(8,128)S(1)}, f32[4,64,128]{2,1,0:T(8,128)S(1)}, u32[]{:S(2)}, u32[]{:S(2)}) collective-permute-start(f32[4,64,128]{2,1,0:T(8,128)S(1)} %get-tuple-element.25), channel_id=1, source_target_pairs={{0,1},{1,2},{2,3},{3,4},{4,5},{5,6},{6,7},{7,8},{8,9},{9,10},{10,1... | collective-permute-start | bytes 393224 | tf_op jit(solution)/shard_map/ppermute | solution.py:16
  21.0 0.7 copy-start.6
  42.5 6.3 %collective-permute-start.3 = (f32[4,64,128]{2,1,0:T(8,128)S(1)}, f32[4,64,128]{2,1,0:T(8,128)S(1)}, u32[]{:S(2)}, u32[]{:S(2)}) collective-permute-start(f32[4,64,128]{2,1,0:T(8,128)S(1)} %get-tuple-element.22), channel_id=1, source_target_pairs={{0,1},{1,2},{2,3},{3,4},{4,5},{5,6},{6,7},{7,8},{8,9},{9,10},{10,1... | collective-permute-start | bytes 393224 | tf_op jit(solution)/shard_map/ppermute | solution.py:16
  46.8 6.3 %collective-permute-start.2 = (f32[4,64,128]{2,1,0:T(8,128)S(1)}, f32[4,64,128]{2,1,0:T(8,128)S(1)}, u32[]{:S(2)}, u32[]{:S(2)}) collective-permute-start(f32[4,64,128]{2,1,0:T(8,128)S(1)} %get-tuple-element.23), channel_id=1, source_target_pairs={{1,0},{2,1},{3,2},{4,3},{5,4},{6,5},{7,6},{8,7},{9,8},{10,9},{11,1... | collective-permute-start | bytes 393224 | tf_op jit(solution)/shard_map/ppermute | solution.py:19
  55.8 17.5 %copy-start.8 = (s32[1,2]{1,0:T(1,128)S(1)}, s32[1,2]{1,0:T(1,128)}, u32[]{:S(2)}) copy-start(s32[1,2]{1,0:T(1,128)} %param.15) | copy-start | bytes 28
  71.4 28.4 %copy-start.1 = (f32[16,64,128]{2,1,0:T(8,128)}, f32[16,64,128]{2,1,0:T(8,128)S(1)}, u32[]{:S(2)}) copy-start(f32[16,64,128]{2,1,0:T(8,128)S(1)} %scatter_fusion.1) | copy-start | bytes 1572868
  71.4 6.4 %collective-permute-start.5 = (f32[4,64,128]{2,1,0:T(8,128)S(1)}, f32[4,64,128]{2,1,0:T(8,128)S(1)}, u32[]{:S(2)}, u32[]{:S(2)}) collective-permute-start(f32[4,64,128]{2,1,0:T(8,128)S(1)} %get-tuple-element.18), channel_id=1, source_target_pairs={{0,1},{1,2},{2,3},{3,4},{4,5},{5,6},{6,7},{7,8},{8,9},{9,10},{10,1... | collective-permute-start | bytes 393224 | tf_op jit(solution)/shard_map/ppermute | solution.py:16
  75.2 6.3 %collective-permute-start.4 = (f32[4,64,128]{2,1,0:T(8,128)S(1)}, f32[4,64,128]{2,1,0:T(8,128)S(1)}, u32[]{:S(2)}, u32[]{:S(2)}) collective-permute-start(f32[4,64,128]{2,1,0:T(8,128)S(1)} %get-tuple-element.19), channel_id=1, source_target_pairs={{1,0},{2,1},{3,2},{4,3},{5,4},{6,5},{7,6},{8,7},{9,8},{10,9},{11,1... | collective-permute-start | bytes 393224 | tf_op jit(solution)/shard_map/ppermute | solution.py:19
  84.2 15.6 %copy-start.5 = (bf16[1,3,16,64,128]{4,3,2,1,0:T(8,128)(2,1)S(1)}, bf16[1,3,16,64,128]{4,3,2,1,0:T(8,128)(2,1)}, u32[]{:S(2)}) copy-start(bf16[1,3,16,64,128]{4,3,2,1,0:T(8,128)(2,1)} %param.12) | copy-start | bytes 2359300
  99.8 1.4 copy-start.2
  99.8 1.4 copy-start.7
Sparse Core Ops, SparseCore 0:
  101.3 118.1 reduce-scatter.1
where the time goes:
time: 335 us
  waiting for transfers between devices  126 us (38%)
  blocking collectives  102 us (30%)
  other arithmetic  60 us (18%)
  starting transfers between devices  21.5 us (6%)
  between operations  14.4 us (4%)
  local copies, waits for them, and re-layouts  9.37 us (3%)
    reduce_scatter x1, waiting for transfers between devices, body(): lax.psum_scatter(image_rows, 'shot', scatter_dimension=0, tiled=True)  118 us
    psum x1, blocking collectives, body(): lax.psum(partial_grad, ('shot', 'slab')) * (1.0 / math.sqrt(latent_cells))  102 us
    scatter-add x3, other arithmetic, inject(): field.at[local_x, receivers[0, 1], receivers[0, 2]].add(values, mode='drop')  46.7 us
    ppermute x3, starting transfers between devices, extended(): lax.ppermute(lax.slice_in_dim(block, 0, width, axis=dim), axis, backward)  13.3 us
    ppermute x3, starting transfers between devices, extended(): lax.ppermute(lax.slice_in_dim(block, block.shape[dim] - width, None, axis...  8.19 us
    add x3, other arithmetic, body(): advanced = 2.0 * current - previous + courant * laplace(pad_sides(padded))  7.87 us
    ppermute x3, waiting for transfers between devices, extended(): lax.ppermute(lax.slice_in_dim(block, 0, width, axis=dim), axis, backward)  7.76 us
  transfers between devices with their start and end apart: 7, of which 4 were waited for; matrix products, arithmetic and copies ran while one was open for 1% of the time, Pallas kernels for 0%

commit v1 on v0

--- a/solution.py
+++ b/solution.py
@@ -6,6 +6,10 @@
 
 STEPS = 3
 stencil_weights = (-205.0 / 72.0, 8.0 / 5.0, -1.0 / 5.0, 8.0 / 315.0, -1.0 / 560.0)
+
+
+def row_place(mine_x):
+    return lax.psum(lax.psum(mine_x, axis_name="shot"), axis_name="slab")
 
 
 def extended(block, sides, width):
@@ -90,7 +94,7 @@
     latent_cells = (
         latent.shape[0] * lax.axis_size("slab") * latent.shape[1] * lax.axis_size("shot") * half_z
     )
-    weight_grad = lax.psum(partial_grad, ("shot", "slab")) * (1.0 / math.sqrt(latent_cells))
+    weight_grad = row_place(partial_grad) * (1.0 / math.sqrt(latent_cells))
     return (current[None], previous[None], latent_grad, weight_grad)
 
 

time: 335 us -> 355 us (1.060)
  blocking collectives: 102 us -> 121 us
    psum x1 -> x2, blocking collectives: 102 us -> 121 us  [row_place(): return lax.psum(lax.psum(mine_x, axis_name='shot'), axis_name='slab')]
where the time goes in v1:
time: 355 us
  waiting for transfers between devices  126 us (35%)
  blocking collectives  121 us (34%)
  other arithmetic  61.4 us (17%)
  starting transfers between devices  21.6 us (6%)
  between operations  14.4 us (4%)
  local copies, waits for them, and re-layouts  8.71 us (2%)
    psum x2, blocking collectives, row_place(): return lax.psum(lax.psum(mine_x, axis_name='shot'), axis_name='slab')  121 us
    reduce_scatter x1, waiting for transfers between devices, body(): lax.psum_scatter(image_rows, 'shot', scatter_dimension=0, tiled=True)  118 us
    scatter-add x3, other arithmetic, inject(): field.at[local_x, receivers[0, 1], receivers[0, 2]].add(values, mode='drop')  46.7 us
    ppermute x3, starting transfers between devices, extended(): lax.ppermute(lax.slice_in_dim(block, 0, width, axis=dim), axis, backward)  13.3 us
    ppermute x3, starting transfers between devices, extended(): lax.ppermute(lax.slice_in_dim(block, block.shape[dim] - width, None, axis...  8.3 us
    add x3, other arithmetic, body(): advanced = 2.0 * current - previous + courant * laplace(pad_sides(padded))  7.85 us
    ppermute x3, waiting for transfers between devices, extended(): lax.ppermute(lax.slice_in_dim(block, 0, width, axis=dim), axis, backward)  7.75 us
  transfers between devices with their start and end apart: 7, of which 4 were waited for; matrix products, arithmetic and copies ran while one was open for 1% of the time, Pallas kernels for 0%

profile of v1, /device:TPU:1, one launch (start us, length us, event | category | flops | bytes accessed | tf_op | source)
XLA Modules:
  0.0 354.7 jit_solution(237768908364594585)
XLA Ops:
  7.2 1.1 slice_bitcast_fusion.1
  8.3 8.8 %collective-permute-start = (f32[4,64,128]{2,1,0:T(8,128)S(1)}, f32[4,64,128]{2,1,0:T(8,128)S(1)}, u32[]{:S(2)}, u32[]{:S(2)}) collective-permute-start(f32[4,64,128]{2,1,0:T(8,128)S(1)} %get-tuple-element.24), channel_id=1, source_target_pairs={{1,0},{2,1},{3,2},{4,3},{5,4},{6,5},{7,6},{8,7},{9,8},{10,9},{11,1... | collective-permute-start | bytes 393224 | tf_op jit(solution)/shard_map/ppermute | solution.py:23
  17.1 1.9 collective-permute-start.1
  19.0 0.7 fusion.67
  19.8 0.7 or_select_fusion
  21.0 1.6 select_maximum_fusion.4
  22.6 3.7 %fusion.13 = f32[16,64,128]{2,1,0:T(8,128)S(1)} fusion(f32[16,64,128]{2,1,0:T(8,128)S(1)} %copy-done.3, f32[16,64,128]{2,1,0:T(8,128)S(1)} %bitcast.63, f32[4,64,128]{2,1,0:T(8,128)} %collective-permute-done.1, f32[4,64,128]{2,1,0:T(8,128)S(1)} %collective-permute-done, f32[24,72,136]{2,1,0:T(8,128)S(1)} %select_maximum_fusion.4, f32[1,16,64,128]{3,2,1,0:T(8,128)} %param.10), kind=kLoop, calls=%fused_computation.40 | loop fusion | flops 5373952 | bytes 10747904 | tf_op jit(solution)/shard_map/add | solution.py:69
  26.2 15.6 %scatter_fusion = f32[16,64,128]{2,1,0:T(8,128)S(1)} fusion(f32[16,64,128]{2,1,0:T(8,128)S(1)} %fusion.13, s32[256]{0:T(256)S(1)} %bitcast.56, f32[256]{0:T(256)S(1)} %bitcast.69), kind=kCustom, calls=%fused_computation | custom fusion | flops 256 | bytes 6144 | tf_op jit(solution)/shard_map/scatter-add | solution.py:58
  41.8 4.5 %collective-permute-start.3 = (f32[4,64,128]{2,1,0:T(8,128)S(1)}, f32[4,64,128]{2,1,0:T(8,128)S(1)}, u32[]{:S(2)}, u32[]{:S(2)}) collective-permute-start(f32[4,64,128]{2,1,0:T(8,128)S(1)} %get-tuple-element.22), channel_id=1, source_target_pairs={{0,1},{1,2},{2,3},{3,4},{4,5},{5,6},{6,7},{7,8},{8,9},{9,10},{10,1... | collective-permute-start | bytes 393224 | tf_op jit(solution)/shard_map/ppermute | solution.py:20
  46.3 1.9 collective-permute-start.2
  48.4 4.2 %collective-permute-done.2 = f32[4,64,128]{2,1,0:T(8,128)S(1)} collective-permute-done((f32[4,64,128]{2,1,0:T(8,128)S(1)}, f32[4,64,128]{2,1,0:T(8,128)S(1)}, u32[]{:S(2)}, u32[]{:S(2)}) %collective-permute-start.2) | collective-permute-done | bytes 131104 | tf_op jit(solution)/shard_map/ppermute | solution.py:23
  52.6 0.5 select_maximum_fusion.2
  53.1 2.1 fusion.46
  55.2 15.6 %scatter_fusion.1 = f32[16,64,128]{2,1,0:T(8,128)S(1)} fusion(f32[16,64,128]{2,1,0:T(8,128)S(1)} %fusion.46, s32[256]{0:T(256)S(1)} %bitcast.57, f32[256]{0:T(256)S(1)} %bitcast.68), kind=kCustom, calls=%fused_computation.1 | custom fusion | flops 256 | bytes 6144 | tf_op jit(solution)/shard_map/scatter-add | solution.py:58
  70.8 1.9 collective-permute-start.5
  72.8 0.6 fusion.68
  73.4 1.3 compare_and_fusion
  74.7 2.6 collective-permute-start.4
  77.4 3.5 collective-permute-done.4
  81.0 0.5 select_maximum_fusion
  81.5 2.1 fusion.36
  83.6 15.6 %scatter_fusion.2 = f32[16,64,128]{2,1,0:T(8,128)S(1)} fusion(f32[16,64,128]{2,1,0:T(8,128)S(1)} %fusion.36, s32[256]{0:T(256)S(1)} %bitcast.58, f32[256]{0:T(256)S(1)} %bitcast.67), kind=kCustom, calls=%fused_computation.2 | custom fusion | flops 256 | bytes 6144 | tf_op jit(solution)/shard_map/scatter-add | solution.py:58
  99.2 1.6 fusion.58
  100.9 1.1 copy.23
  102.2 118.1 %reduce-scatter.2.cloned.1.call-done = f32[4,16,128]{2,1,0:T(8,128)} async-done(((f32[64,16,128]{2,1,0:T(8,128)}), f32[4,16,128]{2,1,0:T(8,128)}) %reduce-scatter.2.cloned.1.call-update) | async-done | bytes 32784 | tf_op jit(solution)/shard_map/reduce_scatter | solution.py:79
  220.3 2.8 reshape.124
  223.2 0.7 copy.24
  223.9 1.0 convolution_bitcast_fusion
  225.1 1.0 reshape.151
  226.4 44.3 %psum.14 = f32[64,8]{0,1:T(8,128)S(1)} all-reduce(f32[64,8]{0,1:T(8,128)S(1)} %convolution_bitcast_fusion.1), channel_id=1, replica_groups=mesh['shot'=16,'slab'=32] {'shot'}, use_global_device_ids=true, to_apply=%region_4.5 | all-reduce | flops 512 | bytes 4096 | tf_op jit(solution)/shard_map/psum | solution.py:12
  270.6 76.7 %psum.15 = f32[64,8]{0,1:T(8,128)S(1)} all-reduce(f32[64,8]{0,1:T(8,128)S(1)} %psum.14), channel_id=1, replica_groups=mesh['shot'=16,'slab'=32] {'slab'}, use_global_device_ids=true, to_apply=%region_5.6 | all-reduce | flops 512 | bytes 4096 | tf_op jit(solution)/shard_map/psum | solution.py:12
  347.3 0.6 broadcast_multiply_fusion
  (31 shorter events, 1.6 us)
Async XLA Ops:
  7.2 216.7 %copy-start = (f32[64,8]{0,1:T(8,128)S(1)}, f32[64,8]{0,1:T(8,128)}, u32[]{:S(2)}) copy-start(f32[64,8]{0,1:T(8,128)} %param.17) | copy-start | bytes 6148
  7.2 15.4 %copy-start.4 = (f32[1,16,64,128]{3,2,1,0:T(8,128)S(1)}, f32[1,16,64,128]{3,2,1,0:T(8,128)}, u32[]{:S(2)}) copy-start(f32[1,16,64,128]{3,2,1,0:T(8,128)} %param.9) | copy-start | bytes 1572868
  7.2 15.4 %copy-start.3 = (f32[16,64,128]{2,1,0:T(8,128)S(1)}, f32[16,64,128]{2,1,0:T(8,128)}, u32[]{:S(2)}) copy-start(f32[16,64,128]{2,1,0:T(8,128)} %param.11) | copy-start | bytes 1572868
  7.2 213.1 %reduce-scatter.2.cloned.1.call-start = ((), (), s32[]{:S(2)}) async-start(), calls=%async_computation.1 | async-start | bytes 557056 | tf_op jit(solution)/shard_map/reduce_scatter | solution.py:79
  8.3 12.2 %collective-permute-start = (f32[4,64,128]{2,1,0:T(8,128)S(1)}, f32[4,64,128]{2,1,0:T(8,128)S(1)}, u32[]{:S(2)}, u32[]{:S(2)}) collective-permute-start(f32[4,64,128]{2,1,0:T(8,128)S(1)} %get-tuple-element.24), channel_id=1, source_target_pairs={{1,0},{2,1},{3,2},{4,3},{5,4},{6,5},{7,6},{8,7},{9,8},{10,9},{11,1... | collective-permute-start | bytes 393224 | tf_op jit(solution)/shard_map/ppermute | solution.py:23
  17.1 3.9 %collective-permute-start.1 = (f32[4,64,128]{2,1,0:T(8,128)S(1)}, f32[4,64,128]{2,1,0:T(8,128)}, u32[]{:S(2)}, u32[]{:S(2)}) collective-permute-start(f32[4,64,128]{2,1,0:T(8,128)S(1)} %get-tuple-element.25), channel_id=1, source_target_pairs={{0,1},{1,2},{2,3},{3,4},{4,5},{5,6},{6,7},{7,8},{8,9},{9,10},{10,1... | collective-permute-start | bytes 393224 | tf_op jit(solution)/shard_map/ppermute | solution.py:20
  41.8 6.4 %collective-permute-start.3 = (f32[4,64,128]{2,1,0:T(8,128)S(1)}, f32[4,64,128]{2,1,0:T(8,128)S(1)}, u32[]{:S(2)}, u32[]{:S(2)}) collective-permute-start(f32[4,64,128]{2,1,0:T(8,128)S(1)} %get-tuple-element.22), channel_id=1, source_target_pairs={{0,1},{1,2},{2,3},{3,4},{4,5},{5,6},{6,7},{7,8},{8,9},{9,10},{10,1... | collective-permute-start | bytes 393224 | tf_op jit(solution)/shard_map/ppermute | solution.py:20
  46.3 6.3 %collective-permute-start.2 = (f32[4,64,128]{2,1,0:T(8,128)S(1)}, f32[4,64,128]{2,1,0:T(8,128)S(1)}, u32[]{:S(2)}, u32[]{:S(2)}) collective-permute-start(f32[4,64,128]{2,1,0:T(8,128)S(1)} %get-tuple-element.23), channel_id=1, source_target_pairs={{1,0},{2,1},{3,2},{4,3},{5,4},{6,5},{7,6},{8,7},{9,8},{10,9},{11,1... | collective-permute-start | bytes 393224 | tf_op jit(solution)/shard_map/ppermute | solution.py:23
  55.2 17.5 %copy-start.6 = (s32[1,2]{1,0:T(1,128)S(1)}, s32[1,2]{1,0:T(1,128)}, u32[]{:S(2)}) copy-start(s32[1,2]{1,0:T(1,128)} %param.15) | copy-start | bytes 28
  70.8 28.4 %copy-start.1 = (f32[16,64,128]{2,1,0:T(8,128)}, f32[16,64,128]{2,1,0:T(8,128)S(1)}, u32[]{:S(2)}) copy-start(f32[16,64,128]{2,1,0:T(8,128)S(1)} %scatter_fusion.1) | copy-start | bytes 1572868
  70.8 6.4 %collective-permute-start.5 = (f32[4,64,128]{2,1,0:T(8,128)S(1)}, f32[4,64,128]{2,1,0:T(8,128)S(1)}, u32[]{:S(2)}, u32[]{:S(2)}) collective-permute-start(f32[4,64,128]{2,1,0:T(8,128)S(1)} %get-tuple-element.18), channel_id=1, source_target_pairs={{0,1},{1,2},{2,3},{3,4},{4,5},{5,6},{6,7},{7,8},{8,9},{9,10},{10,1... | collective-permute-start | bytes 393224 | tf_op jit(solution)/shard_map/ppermute | solution.py:20
  74.7 6.3 %collective-permute-start.4 = (f32[4,64,128]{2,1,0:T(8,128)S(1)}, f32[4,64,128]{2,1,0:T(8,128)S(1)}, u32[]{:S(2)}, u32[]{:S(2)}) collective-permute-start(f32[4,64,128]{2,1,0:T(8,128)S(1)} %get-tuple-element.19), channel_id=1, source_target_pairs={{1,0},{2,1},{3,2},{4,3},{5,4},{6,5},{7,6},{8,7},{9,8},{10,9},{11,1... | collective-permute-start | bytes 393224 | tf_op jit(solution)/shard_map/ppermute | solution.py:23
  99.2 2.8 copy-start.2
  99.2 2.8 copy-start.5
Sparse Core Ops, SparseCore 0:
  102.1 118.1 reduce-scatter.1
